TPU v7x, 128 devices: a whole 4x4x4 slice. The times are simulated.
128 devices in a mesh: section: 2 (over y_hi), expert: 8 (over z, core), hid: 8 (over x, y_lo).
Axes of the slice: x: 4, y: 4 (y_hi: 2, y_lo: 2; y = y_hi * 2 + y_lo), z: 4, core: 2. Of those that a mesh axis runs over, the one named last changes fastest.
Arguments:
- saved_input: bfloat16 [2, 1024, 4096], P('section', 'expert', 'hid'), may hold values from -6 to 6
- cotangent: bfloat16 [2, 1024, 4096], P('section', 'expert', 'hid'), may hold values from -6 to 6
- next_input: bfloat16 [2, 1024, 4096], P('section', 'expert', 'hid'), may hold values from -6 to 6
- routes_saved: int32 [2, 1024, 2], P('section', 'expert'), may hold values from 0 to 7, all different within a row; in each aligned block of 128 rows (0 to 127, 128 to 255, ..., all dimensions but the last counted through in order) at most 48 rows name the same one
- routes_next: int32 [2, 1024, 2], P('section', 'expert'), may hold values from 0 to 7, all different within a row; in each aligned block of 128 rows (0 to 127, 128 to 255, ..., all dimensions but the last counted through in order) at most 48 rows name the same one
- norm_gain: float32 [2, 4096], P('section', 'hid'), may hold values from 0.1 to 1.9
- router: float32 [2, 4096, 8], P('section', 'hid'), may hold values from -0.18 to 0.18
- expert_gate: bfloat16 [2, 8, 4096, 7168], P('section', 'expert', None, 'hid'), may hold values from -0.09375 to 0.09375
- expert_up: bfloat16 [2, 8, 4096, 7168], P('section', 'expert', None, 'hid'), may hold values from -0.09375 to 0.09375
- expert_down: bfloat16 [2, 8, 7168, 4096], P('section', 'expert', 'hid'), may hold values from -0.0625 to 0.0625
Outputs:
- leaving: bfloat16 [2, 1024, 4096], P('section', 'expert', 'hid')
- arriving: bfloat16 [2, 1024, 4096], P('section', 'expert', 'hid')
Inputs may be any that keep to these rules, and one draw needn't show every extreme that they name: `routes_saved`: A token's two ids differ. In each aligned block of 128 tokens of a section no expert is named by more than 48 tokens, and some block names some expert exactly 48 times. `routes_next`: A token's two ids differ. In each aligned block of 128 tokens of a section no expert is named by more than 48 tokens, and some block names some expert exactly 48 times.
All inputs are finite; a program needn't handle non-finite values.
Results may differ from a plain program's by a relative error of at most 0.0052.
Values may be sent and summed in bfloat16 or wider, within the bound.
No kernel may reach another device: no remote copies, remote signals or barrier semaphores. Data moves between devices by JAX's collectives and lax.ppermute only.
A program may use at most 128 MiB of HBM per device.

v0:
```python
import jax
import jax.numpy as jnp
from jax import lax
from jax.sharding import PartitionSpec as P

EPSILON = 1e-05
HIGHEST = lax.Precision.HIGHEST
CONTRACT = (((1,), (1,)), ((), ()))


def partner(block, axis, bit):
    count = lax.axis_size(axis)
    route = []
    for low in range(count):
        high = low | 1 << bit
        if high != low and high < count:
            route += [(low, high), (high, low)]
    return lax.ppermute(block, axis, route)


def norm_terms(values, gain, table):
    squares = jnp.sum(values * values, axis=1)
    partial_value = jnp.dot(values * gain[None, :], table, precision=HIGHEST)
    return (squares, partial_value)


def finish_norm(values, squares, partial_value, gain, width):
    scale = lax.rsqrt(squares / width + EPSILON)
    normed = (values * scale[:, None] * gain[None, :]).astype(jnp.bfloat16)
    return (scale, normed, scale[:, None] * partial_value)


def placing(routes, logits, capacity):
    experts = logits.shape[1]
    tokens = routes.shape[0]
    labels = jnp.arange(experts, dtype=jnp.int32)
    flat_ids = routes.reshape(-1)
    onehot = (flat_ids[:, None] == labels[None, :]).astype(jnp.int32)
    ranked = jnp.cumsum(onehot, axis=0) - onehot
    places = jnp.sum(ranked * onehot, axis=1)
    targets = (flat_ids * capacity + places).reshape(tokens, 2)
    first_hit = (routes[:, 0:1] == labels[None, :]).astype(jnp.float32)
    second_hit = (routes[:, 1:2] == labels[None, :]).astype(jnp.float32)
    first_logit = jnp.sum(logits * first_hit, axis=1)
    second_logit = jnp.sum(logits * second_hit, axis=1)
    first_prob = jax.nn.sigmoid(first_logit - second_logit)
    second_prob = jax.nn.sigmoid(second_logit - first_logit)
    all_slots = jnp.arange(experts * capacity, dtype=jnp.int32)
    slot_map = jnp.any(targets[None, :, :] == all_slots[:, None, None], axis=2).astype(jnp.bfloat16)
    return (targets, first_prob, second_prob, first_hit - second_hit, slot_map)


def row_buffer(slot_map, rows):
    return jnp.dot(slot_map, rows, preferred_element_type=jnp.float32).astype(jnp.bfloat16)


def blend(rows, targets, first_prob, second_prob):
    return first_prob[:, None] * rows[targets[:, 0]] + second_prob[:, None] * rows[targets[:, 1]]


def add_products(matrices, pieces):
    gate_matrix, up_matrix, down_matrix = matrices
    saved_rows, cot_rows, next_rows = pieces
    gate_saved = jnp.dot(saved_rows, gate_matrix, preferred_element_type=jnp.float32)
    up_saved = jnp.dot(saved_rows, up_matrix, preferred_element_type=jnp.float32)
    grad_hidden = lax.dot_general(
        cot_rows, down_matrix, CONTRACT, preferred_element_type=jnp.float32
    )
    gate_next = jnp.dot(next_rows, gate_matrix, preferred_element_type=jnp.float32)
    up_next = jnp.dot(next_rows, up_matrix, preferred_element_type=jnp.float32)
    return (gate_saved, up_saved, grad_hidden, gate_next, up_next)


def per_device(
    saved_input,
    cotangent,
    next_input,
    routes_saved,
    routes_next,
    norm_gain,
    router,
    expert_gate,
    expert_up,
    expert_down,
):
    gain = norm_gain[0]
    table = router[0]
    gate_matrix = expert_gate[0, 0]
    up_matrix = expert_up[0, 0]
    down_matrix = expert_down[0, 0]
    matrices = (gate_matrix, up_matrix, down_matrix)
    width = gate_matrix.shape[0]
    cot_rows = cotangent[0]
    values_saved = saved_input[0].astype(jnp.float32)
    values_next = next_input[0].astype(jnp.float32)
    squares_saved, partial_saved = norm_terms(values_saved, gain, table)
    squares_next, partial_next = norm_terms(values_next, gain, table)
    squares_saved, partial_saved, squares_next, partial_next = lax.psum(
        (squares_saved, partial_saved, squares_next, partial_next), "hid"
    )
    scale_saved, normed_saved, logits_saved = finish_norm(
        values_saved, squares_saved, partial_saved, gain, width
    )
    scale_next, normed_next, logits_next = finish_norm(
        values_next, squares_next, partial_next, gain, width
    )
    tokens = values_saved.shape[0]
    experts = lax.axis_size("expert")
    capacity = 3 * tokens // experts
    targets_saved, first_saved, second_saved, diff_saved, map_saved = placing(
        routes_saved[0], logits_saved, capacity
    )
    targets_next, first_next, second_next, diff_next, map_next = placing(
        routes_next[0], logits_next, capacity
    )
    packed = (
        row_buffer(map_saved, normed_saved),
        row_buffer(map_saved, cot_rows),
        row_buffer(map_next, normed_next),
    )
    moved = (
        lax.all_to_all(packed[0], "expert", split_axis=0, concat_axis=0, tiled=True),
        lax.all_to_all(packed[1], "expert", split_axis=0, concat_axis=0, tiled=True),
        lax.all_to_all(packed[2], "expert", split_axis=0, concat_axis=0, tiled=True),
    )
    sums = add_products(
        matrices,
        (
            lax.all_gather(moved[0], "hid", axis=1, tiled=True),
            lax.all_gather(moved[1], "hid", axis=1, tiled=True),
            lax.all_gather(moved[2], "hid", axis=1, tiled=True),
        ),
    )
    gate_saved, up_saved, grad_hidden, gate_next, up_next = sums
    sig_saved = jax.nn.sigmoid(gate_saved)
    silu_saved = gate_saved * sig_saved
    hidden_saved = (silu_saved * up_saved).astype(jnp.bfloat16)
    dot_terms = jnp.sum(grad_hidden * hidden_saved.astype(jnp.float32), axis=1)
    row_dots = lax.psum(dot_terms, "hid")
    grad_gate = (
        grad_hidden * up_saved * (sig_saved * (1.0 + gate_saved * (1.0 - sig_saved)))
    ).astype(jnp.bfloat16)
    grad_up = (grad_hidden * silu_saved).astype(jnp.bfloat16)
    back_part = lax.dot_general(
        grad_gate, gate_matrix, CONTRACT, preferred_element_type=jnp.float32
    ) + lax.dot_general(grad_up, up_matrix, CONTRACT, preferred_element_type=jnp.float32)
    silu_next = gate_next * jax.nn.sigmoid(gate_next)
    hidden_next = (silu_next * up_next).astype(jnp.bfloat16)
    out_part = jnp.dot(hidden_next, down_matrix, preferred_element_type=jnp.float32)
    back_sum, out_sum = (
        lax.psum_scatter(back_part, "hid", scatter_dimension=1, tiled=True),
        lax.psum_scatter(out_part, "hid", scatter_dimension=1, tiled=True),
    )
    back_home, dots_home, out_home = (
        lax.all_to_all(back_sum, "expert", split_axis=0, concat_axis=0, tiled=True),
        lax.all_to_all(row_dots, "expert", split_axis=0, concat_axis=0, tiled=True),
        lax.all_to_all(out_sum, "expert", split_axis=0, concat_axis=0, tiled=True),
    )
    mixed_saved = blend(back_home, targets_saved, first_saved, second_saved)
    branch_next = blend(out_home, targets_next, first_next, second_next)
    forward_out = (values_next + branch_next).astype(jnp.bfloat16)
    grad_logit = (
        (dots_home[targets_saved[:, 0]] - dots_home[targets_saved[:, 1]])
        * first_saved
        * second_saved
    )
    grad_normed = mixed_saved + jnp.dot(
        grad_logit[:, None] * diff_saved, table.T, precision=HIGHEST
    )
    scaled_grad = grad_normed * gain[None, :]
    inner = lax.psum(jnp.sum(scaled_grad * values_saved, axis=1), "hid")
    cube = scale_saved * scale_saved * scale_saved
    grad_input = (
        cot_rows.astype(jnp.float32)
        + scale_saved[:, None] * scaled_grad
        - values_saved * cube[:, None] * (inner / width)[:, None]
    )
    grad_input = grad_input.astype(jnp.bfloat16)
    first_section = lax.axis_index("section") == 0
    outgoing = jnp.where(first_section, forward_out, grad_input)
    leaving = jnp.where(first_section, grad_input, forward_out)
    arriving = partner(outgoing, "section", 0)
    return (leaving[None], arriving[None])


def solution(mesh):
    placed = (
        P("section", "expert", "hid"),
        P("section", "expert", "hid"),
        P("section", "expert", "hid"),
        P("section", "expert", None),
        P("section", "expert", None),
        P("section", "hid"),
        P("section", "hid", None),
        P("section", "expert", None, "hid"),
        P("section", "expert", None, "hid"),
        P("section", "expert", "hid", None),
    )
    return jax.shard_map(
        per_device,
        mesh=mesh,
        in_specs=placed,
        out_specs=(P("section", "expert", "hid"), P("section", "expert", "hid")),
        check_vma=False,
    )
```

profile of v0, /device:TPU:0, one launch (start us, length us, event | category | flops | bytes accessed | tf_op | source)
XLA Modules:
  0.0 648.1 jit_solution(6616434694353465557)
XLA Ops:
  7.2 0.8 copy.58
  8.3 1.0 fusion.39
  9.4 19.8 %psum.42 = f32[128]{0:T(128)S(1)} all-reduce(f32[128]{0:T(128)S(1)} %fusion.39), channel_id=1, replica_groups=mesh['section'=2,'expert'=8,'hid'=8] {'hid'}, use_global_device_ids=true, to_apply=%region_1.0 | all-reduce | flops 128 | bytes 1024 | tf_op jit(solution)/shard_map/psum | solution.py:98
  29.2 0.6 reduce-window.14
  30.3 0.7 add_bitcast_fusion.1
  31.1 1.2 convolution_convert_fusion.1
  32.3 14.2 %all_to_all.72 = bf16[8,48,512]{2,1,0:T(8,128)(2,1)} all-to-all(bf16[8,48,512]{2,1,0:T(8,128)(2,1)S(1)} %bitcast.152), channel_id=1, replica_groups=mesh['section'=2,'expert'=8,'hid'=8] {'expert'}, dimensions={0} | all-to-all | bytes 786432 | tf_op jit(solution)/shard_map/all_to_all | solution.py:122
  46.6 0.2 convolution_convert_fusion.2
  46.8 12.0 %all_to_all.73 = bf16[8,48,512]{2,1,0:T(8,128)(2,1)} all-to-all(bf16[8,48,512]{2,1,0:T(8,128)(2,1)S(1)} %bitcast.150), channel_id=1, replica_groups=mesh['section'=2,'expert'=8,'hid'=8] {'expert'}, dimensions={0} | all-to-all | bytes 786432 | tf_op jit(solution)/shard_map/all_to_all | solution.py:123
  58.9 54.5 %all-gather.6.cloned.1.call-done = bf16[384,4096]{1,0:T(8,128)(2,1)} async-done(((bf16[384,512]{1,0:T(8,128)(2,1)}), bf16[384,4096]{1,0:T(8,128)(2,1)}) %all-gather.6.cloned.1.call-update) | async-done | bytes 3145744 | tf_op jit(solution)/shard_map/all_gather | solution.py:129
  113.5 9.0 %fusion.4 = f32[384,896]{1,0:T(8,128)S(1)} fusion(bf16[384,4096]{1,0:T(8,128)(2,1)} %all-gather.6.cloned.1.call-done, bf16[1,1,4096,896]{3,2,1,0:T(8,128)(2,1)} %param.17), kind=kOutput, calls=%fused_computation.10 | convolution fusion | flops 2818572288 | bytes 11862016 | tf_op jit(solution)/shard_map/dot_general | solution.py:64
  122.5 5.7 fusion.10
  128.2 58.1 %all-gather.4.cloned.1.call-done = bf16[384,4096]{1,0:T(8,128)(2,1)} async-done(((bf16[384,512]{1,0:T(8,128)(2,1)}), bf16[384,4096]{1,0:T(8,128)(2,1)}) %all-gather.4.cloned.1.call-update) | async-done | bytes 3145744 | tf_op jit(solution)/shard_map/all_gather | solution.py:130
  186.3 8.5 %multiply_reduce_fusion = (f32[384]{0:T(512)S(1)}, f32[384,896]{1,0:T(8,128)S(1)}) fusion(f32[384,896]{1,0:T(8,128)S(1)} %fusion.10, f32[384,896]{1,0:T(8,128)S(1)} %fusion.4, bf16[384,4096]{1,0:T(8,128)(2,1)} %all-gather.4.cloned.1.call-done, bf16[1,1,896,4096]{3,2,1,0:T(8,128)(2,1)} %param.19), kind=kOutput, calls=%fused_computation.24 | convolution fusion | flops 2821668352 | bytes 14616064 | tf_op jit(solution)/shard_map/dot_general | solution.py:66
  194.8 6.1 fusion.2
  200.9 10.1 %fusion.16 = f32[384,4096]{1,0:T(8,128)} fusion(f32[384,4096]{1,0:T(8,128)S(1)} %fusion.2, bf16[1,1,4096,896]{3,2,1,0:T(8,128)(2,1)} %param.18, f32[384,896]{1,0:T(8,128)S(1)} %get-tuple-element.30, f32[384,896]{1,0:T(8,128)S(1)} %fusion.4), kind=kOutput, calls=%fused_computation.22 | convolution fusion | flops 2822209536 | bytes 22675456 | tf_op jit(solution)/shard_map/dot_general | solution.py:146
  211.0 0.6 copy-done.5
  212.2 0.6 reduce-window.16
  213.6 0.3 fusion.47
  214.0 26.3 %all-reduce.1 = (f32[128,8]{0,1:T(8,128)S(1)}, f32[8,48,1]{1,0,2:T(8,128)}) all-reduce(f32[128,8]{0,1:T(8,128)S(1)} %fusion.47, f32[8,48,1]{1,0,2:T(8,128)S(1)} %all_to_all.57), channel_id=1, replica_groups=mesh['section'=2,'expert'=8,'hid'=8] {'hid'}, use_global_device_ids=true, to_apply=%region_2.0 | all-reduce | flops 1408 | bytes 11264 | tf_op jit(solution)/shard_map/psum | solution.py:98
  240.3 4.5 all-to-all-start.3
  245.0 5.0 all-to-all-done.3
  250.0 92.7 %reduce-scatter.3.cloned.1.call-done = f32[384,512]{1,0:T(8,128)} async-done(((f32[384,4096]{1,0:T(8,128)}), f32[384,512]{1,0:T(8,128)}) %reduce-scatter.3.cloned.1.call-update) | async-done | bytes 786448 | tf_op jit(solution)/shard_map/reduce_scatter | solution.py:151
  342.7 4.4 all-to-all-start.2
  347.3 0.3 fusion.54
  347.7 0.5 broadcast.217
  348.2 0.7 reduce.23
  349.0 1.3 gather_fusion.3
  350.2 1.3 gather_fusion.2
  351.5 8.8 %all-to-all-done.2 = f32[8,48,512]{2,1,0:T(8,128)S(1)} async-done(((f32[8,48,512]{2,1,0:T(8,128)}), f32[8,48,512]{2,1,0:T(8,128)S(1)}, u32[]{:S(2)}, u32[]{:S(2)}) %all-to-all-start.2) | async-done | bytes 786464 | tf_op jit(solution)/shard_map/all_to_all | solution.py:155
  360.3 0.8 gather_fusion.1
  361.1 0.8 gather_fusion
  361.8 0.5 fusion.45
  362.4 18.8 %all-reduce = (f32[128]{0:T(128)S(1)}, f32[128]{0:T(128)S(1)}, f32[128,8]{0,1:T(8,128)S(1)}) all-reduce(f32[128]{0:T(128)S(1)} %get-tuple-element.31, f32[128]{0:T(128)S(1)} %fusion.49, f32[128,8]{0,1:T(8,128)S(1)} %fusion.54), channel_id=1, replica_groups=mesh['section'=2,'expert'=8,'hid'=8] {'hid'}, use_global_device_ids=true, to_apply=%region_13.14 | all-reduce | flops 1280 | bytes 10240 | tf_op jit(solution)/shard_map/psum | solution.py:171
  381.1 0.3 convolution_convert_fusion
  381.5 12.0 %all_to_all.74 = bf16[8,48,512]{2,1,0:T(8,128)(2,1)} all-to-all(bf16[8,48,512]{2,1,0:T(8,128)(2,1)S(1)} %bitcast.151), channel_id=1, replica_groups=mesh['section'=2,'expert'=8,'hid'=8] {'expert'}, dimensions={0} | all-to-all | bytes 786432 | tf_op jit(solution)/shard_map/all_to_all | solution.py:124
  393.6 67.0 %all-gather.8.cloned.1.call-done = bf16[384,4096]{1,0:T(8,128)(2,1)} async-done(((bf16[384,512]{1,0:T(8,128)(2,1)}), bf16[384,4096]{1,0:T(8,128)(2,1)}) %all-gather.8.cloned.1.call-update) | async-done | bytes 3145744 | tf_op jit(solution)/shard_map/all_gather | solution.py:131
  460.6 8.0 %fusion = f32[384,896]{1,0:T(8,128)S(1)} fusion(bf16[384,4096]{1,0:T(8,128)(2,1)} %all-gather.8.cloned.1.call-done, bf16[1,1,4096,896]{3,2,1,0:T(8,128)(2,1)} %param.17), kind=kOutput, calls=%fused_computation.6 | convolution fusion | flops 2818572288 | bytes 11862016 | tf_op jit(solution)/shard_map/dot_general | solution.py:69
  468.6 15.4 %fusion.12 = f32[384,4096]{1,0:T(8,128)} fusion(bf16[1,1,896,4096]{3,2,1,0:T(8,128)(2,1)} %param.19, bf16[384,4096]{1,0:T(8,128)(2,1)} %all-gather.8.cloned.1.call-done, bf16[1,1,4096,896]{3,2,1,0:T(8,128)(2,1)} %param.18, f32[384,896]{1,0:T(8,128)S(1)} %fusion), kind=kOutput, calls=%fused_computation.18 | convolution fusion | flops 5639208960 | bytes 25493504 | tf_op jit(solution)/shard_map/dot_general | solution.py:149
  484.4 130.6 %reduce-scatter.5.cloned.1.call-done = f32[384,512]{1,0:T(8,128)} async-done(((f32[384,4096]{1,0:T(8,128)}), f32[384,512]{1,0:T(8,128)}) %reduce-scatter.5.cloned.1.call-update) | async-done | bytes 786448 | tf_op jit(solution)/shard_map/reduce_scatter | solution.py:152
  615.0 4.4 all-to-all-start.5
  619.7 12.9 %all-to-all-done.5 = f32[8,48,512]{2,1,0:T(8,128)S(1)} async-done(((f32[8,48,512]{2,1,0:T(8,128)}), f32[8,48,512]{2,1,0:T(8,128)S(1)}, u32[]{:S(2)}, u32[]{:S(2)}) %all-to-all-start.5) | async-done | bytes 786464 | tf_op jit(solution)/shard_map/all_to_all | solution.py:157
  632.6 0.8 gather_fusion.5
  633.4 0.8 gather_fusion.4
  634.3 2.8 collective-permute-start
  637.1 0.7 select_bitcast_fusion
  637.8 3.2 collective-permute-done
  641.0 0.7 copy.68
  (66 shorter events, 3.8 us)
Async XLA Ops:
  7.2 206.5 %copy-start = (f32[1,512,8]{1,2,0:T(8,128)S(1)}, f32[1,512,8]{1,2,0:T(8,128)}, u32[]{:S(2)}) copy-start(f32[1,512,8]{1,2,0:T(8,128)} %param.16) | copy-start | bytes 49156
  7.2 39.4 %copy-start.3 = (bf16[1,128,512]{2,1,0:T(8,128)(2,1)S(1)}, bf16[1,128,512]{2,1,0:T(8,128)(2,1)}, u32[]{:S(2)}) copy-start(bf16[1,128,512]{2,1,0:T(8,128)(2,1)} %param.11) | copy-start | bytes 393220
  7.2 106.3 %all-gather.6.cloned.1.call-start = ((), (), s32[]{:S(2)}) async-start(), calls=%async_computation.9 | async-start | bytes 3538944 | tf_op jit(solution)/shard_map/all_gather | solution.py:129
  46.5 139.8 %all-gather.4.cloned.1.call-start = ((), (), s32[]{:S(2)}) async-start(), calls=%async_computation.8 | async-start | bytes 3538944 | tf_op jit(solution)/shard_map/all_gather | solution.py:130
  58.9 283.9 %reduce-scatter.3.cloned.1.call-start = ((), (), s32[]{:S(2)}) async-start(), calls=%async_computation.10 | async-start | bytes 7077888 | tf_op jit(solution)/shard_map/reduce_scatter | solution.py:151
  113.5 9.0 %copy-start.6 = (bf16[384,4096]{1,0:T(8,128)(2,1)S(1)}, bf16[384,4096]{1,0:T(8,128)(2,1)}, u32[]{:S(2)}) copy-start(bf16[384,4096]{1,0:T(8,128)(2,1)} %all-gather.6.cloned.1.call-done) | copy-start | bytes 9437188
  211.0 0.7 copy-start.5
  211.0 2.7 copy-start.1
  211.0 2.7 copy-start.4
  211.6 135.6 %copy-start.2 = (bf16[1,128,512]{2,1,0:T(8,128)(2,1)S(1)}, bf16[1,128,512]{2,1,0:T(8,128)(2,1)}, u32[]{:S(2)}) copy-start(bf16[1,128,512]{2,1,0:T(8,128)(2,1)} %param.12) | copy-start | bytes 393220
  240.3 9.7 %all-to-all-start.3 = ((f32[8,48,1]{1,2,0:T(1,128)}), f32[8,48,1]{1,2,0:T(1,128)S(1)}, u32[]{:S(2)}, u32[]{:S(2)}) async-start(f32[8,48,1]{1,2,0:T(1,128)} %bitcast.18), calls=%async_computation.4 | async-start | bytes 8192 | tf_op jit(solution)/shard_map/all_to_all | solution.py:156
  342.7 17.6 %all-to-all-start.2 = ((f32[8,48,512]{2,1,0:T(8,128)}), f32[8,48,512]{2,1,0:T(8,128)S(1)}, u32[]{:S(2)}, u32[]{:S(2)}) async-start(f32[8,48,512]{2,1,0:T(8,128)} %bitcast.153), calls=%async_computation.3 | async-start | bytes 1572864 | tf_op jit(solution)/shard_map/all_to_all | solution.py:155
  347.2 113.5 %all-gather.8.cloned.1.call-start = ((), (), s32[]{:S(2)}) async-start(), calls=%async_computation.11 | async-start | bytes 3538944 | tf_op jit(solution)/shard_map/all_gather | solution.py:131
  393.5 221.5 %reduce-scatter.5.cloned.1.call-start = ((), (), s32[]{:S(2)}) async-start(), calls=%async_computation.12 | async-start | bytes 7077888 | tf_op jit(solution)/shard_map/reduce_scatter | solution.py:152
  615.0 17.6 %all-to-all-start.5 = ((f32[8,48,512]{2,1,0:T(8,128)}), f32[8,48,512]{2,1,0:T(8,128)S(1)}, u32[]{:S(2)}, u32[]{:S(2)}) async-start(f32[8,48,512]{2,1,0:T(8,128)} %bitcast.154), calls=%async_computation.7 | async-start | bytes 1572864 | tf_op jit(solution)/shard_map/all_to_all | solution.py:157
  634.3 6.6 %collective-permute-start = (bf16[128,512]{1,0:T(8,128)(2,1)S(1)}, bf16[128,512]{1,0:T(8,128)(2,1)S(1)}, u32[]{:S(2)}, u32[]{:S(2)}) collective-permute-start(bf16[128,512]{1,0:T(8,128)(2,1)S(1)} %get-tuple-element.19), channel_id=1, source_target_pairs={{0,64},{64,0},{1,65},{65,1},{2,66},{66,2},{3,67},{67,3},{4,68},{68... | collective-permute-start | bytes 393224 | tf_op jit(solution)/shard_map/ppermute | solution.py:18
Sparse Core Ops, SparseCore 0:
  46.6 66.7 all-gather.5
  115.1 71.1 all-gather.3
  211.1 131.5 reduce-scatter.2
  393.7 66.9 all-gather.7
  484.2 130.8 reduce-scatter.4
where the time goes:
time: 649 us; the launch traced here: 648 us
  waiting for transfers between devices  433 us (67%)
  blocking collectives  103 us (16%)
  matrix products  65.6 us (10%)
  starting transfers between devices  16.3 us (3%)
  between operations  14.1 us (2%)
  local copies, waits for them, and re-layouts  10.5 us (2%)
    reduce_scatter x1, waiting for transfers between devices, per_device(): lax.psum_scatter(out_part, 'hid', scatter_dimension=1, tiled=True)  131 us
    reduce_scatter x1, waiting for transfers between devices, per_device(): lax.psum_scatter(back_part, 'hid', scatter_dimension=1, tiled=True)  92.7 us
    all_gather x1, waiting for transfers between devices, per_device(): lax.all_gather(moved[2], 'hid', axis=1, tiled=True)  67 us
    all_gather x1, waiting for transfers between devices, per_device(): lax.all_gather(moved[1], 'hid', axis=1, tiled=True)  58.1 us
    all_gather x1, waiting for transfers between devices, per_device(): lax.all_gather(moved[0], 'hid', axis=1, tiled=True)  54.5 us
    psum x2, blocking collectives, per_device(): lax.psum((squares_saved, partial_saved, squares_next, partial_next), 'hid')  46.2 us
    psum x1, blocking collectives, per_device(): inner = lax.psum(jnp.sum(scaled_grad * values_saved, axis=1), 'hid')  18.8 us
    dot_general x1, matrix products, per_device(): jnp.dot(hidden_next, down_matrix, preferred_element_type=jnp.float32)  15.4 us
  transfers between devices with their start and end apart: 9, of which 9 were waited for; matrix products, arithmetic and copies ran while one was open for 4% of the time, Pallas kernels for 0%

commit v1 on v0

--- a/solution.py
+++ b/solution.py
@@ -168,7 +168,7 @@
         grad_logit[:, None] * diff_saved, table.T, precision=HIGHEST
     )
     scaled_grad = grad_normed * gain[None, :]
-    inner = lax.psum(jnp.sum(scaled_grad * values_saved, axis=1), "hid")
+    inner = jnp.sum(lax.all_gather(jnp.sum(scaled_grad * values_saved, axis=1), "hid"), axis=0)
     cube = scale_saved * scale_saved * scale_saved
     grad_input = (
         cot_rows.astype(jnp.float32)

time: 649 us -> 615 us (0.948)
  waiting for transfers between devices: 433 us -> 390 us
  blocking collectives: 103 us -> 110 us
    psum x1 -> x0, blocking collectives: 18.8 us -> none  [per_device(): inner = lax.psum(jnp.sum(scaled_grad * values_saved, axis=1), 'hid')]
    all_gather x0 -> x1, blocking collectives: none -> 17.6 us  [per_device(): lax.all_gather(jnp.sum(scaled_grad * values_saved, axis=1), 'hid')]
    all_gather x1, waiting for transfers between devices: 67 us -> 50.3 us  [per_device(): lax.all_gather(moved[2], 'hid', axis=1, tiled=True)]
    reduce_scatter x1, waiting for transfers between devices: 131 us -> 115 us  [per_device(): lax.psum_scatter(out_part, 'hid', scatter_dimension=1, tiled=True)]
    all_to_all x1, waiting for transfers between devices: 12.9 us -> 0.01 us  [per_device(): lax.all_to_all(out_sum, 'expert', split_axis=0, concat_axis=0, tiled=True)]
    psum x2, blocking collectives: 46.2 us -> 52.8 us  [per_device(): lax.psum((squares_saved, partial_saved, squares_next, partial_next), 'hid')]
  transfers between devices with their start and end apart: 9 -> 9, of which waited for: 9 -> 8; matrix products, arithmetic and copies ran while one was open for 4% -> 11% of each run, Pallas kernels for 0% -> 0%
where the time goes in v1:
time: 615 us; the launch traced here: 614 us
  waiting for transfers between devices  390 us (63%)
  blocking collectives  110 us (18%)
  matrix products  67 us (11%)
  starting transfers between devices  17.1 us (3%)
  between operations  14.1 us (2%)
  local copies, waits for them, and re-layouts  9.88 us (2%)
    reduce_scatter x1, waiting for transfers between devices, per_device(): lax.psum_scatter(out_part, 'hid', scatter_dimension=1, tiled=True)  115 us
    reduce_scatter x1, waiting for transfers between devices, per_device(): lax.psum_scatter(back_part, 'hid', scatter_dimension=1, tiled=True)  98.6 us
    all_gather x1, waiting for transfers between devices, per_device(): lax.all_gather(moved[1], 'hid', axis=1, tiled=True)  57.2 us
    psum x2, blocking collectives, per_device(): lax.psum((squares_saved, partial_saved, squares_next, partial_next), 'hid')  52.8 us
    all_gather x1, waiting for transfers between devices, per_device(): lax.all_gather(moved[0], 'hid', axis=1, tiled=True)  52.2 us
    all_gather x1, waiting for transfers between devices, per_device(): lax.all_gather(moved[2], 'hid', axis=1, tiled=True)  50.3 us
    all_gather x1, blocking collectives, per_device(): lax.all_gather(jnp.sum(scaled_grad * values_saved, axis=1), 'hid')  17.6 us
    dot_general x1, matrix products, per_device(): jnp.dot(hidden_next, down_matrix, preferred_element_type=jnp.float32)  16 us
  transfers between devices with their start and end apart: 9, of which 8 were waited for; matrix products, arithmetic and copies ran while one was open for 11% of the time, Pallas kernels for 0%

profile of v1, /device:TPU:0, one launch (start us, length us, event | category | flops | bytes accessed | tf_op | source)
XLA Modules:
  0.0 613.9 jit_solution(8567528217669775395)
XLA Ops:
  7.2 0.8 copy.58
  8.3 0.6 reduce-window.14
  8.9 0.2 slice_reduce_fusion.5
  9.5 0.7 add_bitcast_fusion.1
  10.3 1.0 fusion.39
  11.3 19.8 %psum.35 = f32[128]{0:T(128)S(1)} all-reduce(f32[128]{0:T(128)S(1)} %fusion.39), channel_id=1, replica_groups=mesh['section'=2,'expert'=8,'hid'=8] {'hid'}, use_global_device_ids=true, to_apply=%region_1.0 | all-reduce | flops 128 | bytes 1024 | tf_op jit(solution)/shard_map/psum | solution.py:98
  31.1 1.2 convolution_convert_fusion.1
  32.4 14.2 %all_to_all.72 = bf16[8,48,512]{2,1,0:T(8,128)(2,1)} all-to-all(bf16[8,48,512]{2,1,0:T(8,128)(2,1)S(1)} %bitcast.153), channel_id=1, replica_groups=mesh['section'=2,'expert'=8,'hid'=8] {'expert'}, dimensions={0} | all-to-all | bytes 786432 | tf_op jit(solution)/shard_map/all_to_all | solution.py:122
  46.6 0.2 convolution_convert_fusion.2
  46.9 12.0 %all_to_all.73 = bf16[8,48,512]{2,1,0:T(8,128)(2,1)} all-to-all(bf16[8,48,512]{2,1,0:T(8,128)(2,1)S(1)} %bitcast.151), channel_id=1, replica_groups=mesh['section'=2,'expert'=8,'hid'=8] {'expert'}, dimensions={0} | all-to-all | bytes 786432 | tf_op jit(solution)/shard_map/all_to_all | solution.py:123
  59.4 0.6 reduce-window.16
  60.8 0.3 fusion.47
  61.0 0.3 fusion.54
  61.4 52.2 %all-gather.8.cloned.1.call-done = bf16[384,4096]{1,0:T(8,128)(2,1)} async-done(((bf16[384,512]{1,0:T(8,128)(2,1)}), bf16[384,4096]{1,0:T(8,128)(2,1)}) %all-gather.8.cloned.1.call-update) | async-done | bytes 3145744 | tf_op jit(solution)/shard_map/all_gather | solution.py:129
  113.5 8.9 %fusion.4 = f32[384,896]{1,0:T(8,128)S(1)} fusion(bf16[384,4096]{1,0:T(8,128)(2,1)} %all-gather.8.cloned.1.call-done, bf16[1,1,4096,896]{3,2,1,0:T(8,128)(2,1)} %param.17), kind=kOutput, calls=%fused_computation.10 | convolution fusion | flops 2818572288 | bytes 11862016 | tf_op jit(solution)/shard_map/dot_general | solution.py:64
  122.5 6.7 %fusion.10 = f32[384,896]{1,0:T(8,128)} fusion(bf16[384,4096]{1,0:T(8,128)(2,1)S(1)} %copy-done.6, bf16[1,1,4096,896]{3,2,1,0:T(8,128)(2,1)} %param.18), kind=kOutput, calls=%fused_computation.16 | convolution fusion | flops 2818572288 | bytes 11862016 | tf_op jit(solution)/shard_map/dot_general | solution.py:65
  129.2 57.2 %all-gather.6.cloned.1.call-done = bf16[384,4096]{1,0:T(8,128)(2,1)} async-done(((bf16[384,512]{1,0:T(8,128)(2,1)}), bf16[384,4096]{1,0:T(8,128)(2,1)}) %all-gather.6.cloned.1.call-update) | async-done | bytes 3145744 | tf_op jit(solution)/shard_map/all_gather | solution.py:130
  186.3 7.9 %multiply_reduce_fusion = (f32[384]{0:T(512)S(1)}, f32[384,896]{1,0:T(8,128)S(1)}) fusion(f32[384,896]{1,0:T(8,128)} %fusion.10, f32[384,896]{1,0:T(8,128)S(1)} %fusion.4, bf16[384,4096]{1,0:T(8,128)(2,1)} %all-gather.6.cloned.1.call-done, bf16[1,1,896,4096]{3,2,1,0:T(8,128)(2,1)} %param.19), kind=kOutput, calls=%fused_computation.24 | convolution fusion | flops 2821668352 | bytes 14616064 | tf_op jit(solution)/shard_map/dot_general | solution.py:66
  194.3 33.0 %all-reduce = (f32[128,8]{0,1:T(8,128)S(1)}, f32[8,48,1]{1,0,2:T(8,128)}, f32[128]{0:T(128)S(1)}, f32[128,8]{0,1:T(8,128)S(1)}) all-reduce(f32[128,8]{0,1:T(8,128)S(1)} %fusion.47, f32[8,48,1]{1,0,2:T(8,128)S(1)} %all_to_all.57, f32[128]{0:T(128)S(1)} %fusion.49, ...), channel_id=1, replica_groups=mesh['section'=2,'expert'=8,'hid'=8] {'hid'}, use_global_device_ids=true, to_apply=%region_2.0 | all-reduce | flops 2560 | bytes 20480 | tf_op jit(solution)/shard_map/psum | solution.py:98
  227.3 0.3 convolution_convert_fusion
  227.6 13.5 %all_to_all.74 = bf16[8,48,512]{2,1,0:T(8,128)(2,1)} all-to-all(bf16[8,48,512]{2,1,0:T(8,128)(2,1)S(1)} %bitcast.152), channel_id=1, replica_groups=mesh['section'=2,'expert'=8,'hid'=8] {'expert'}, dimensions={0} | all-to-all | bytes 786432 | tf_op jit(solution)/shard_map/all_to_all | solution.py:124
  241.2 0.2 reduce-scatter.3.cloned.1.call-start
  241.4 6.4 %fusion.2 = f32[384,4096]{1,0:T(8,128)S(1)} fusion(bf16[1,1,4096,896]{3,2,1,0:T(8,128)(2,1)} %param.17, f32[384,896]{1,0:T(8,128)S(1)} %fusion.4, f32[384,896]{1,0:T(8,128)S(1)} %get-tuple-element.29, f32[384,896]{1,0:T(8,128)} %fusion.10), kind=kOutput, calls=%fused_computation.8 | convolution fusion | flops 2822012928 | bytes 17760256 | tf_op jit(solution)/shard_map/dot_general | solution.py:144
  247.8 10.1 %fusion.16 = f32[384,4096]{1,0:T(8,128)} fusion(f32[384,4096]{1,0:T(8,128)S(1)} %fusion.2, bf16[1,1,4096,896]{3,2,1,0:T(8,128)(2,1)} %param.18, f32[384,896]{1,0:T(8,128)S(1)} %get-tuple-element.29, f32[384,896]{1,0:T(8,128)S(1)} %fusion.4), kind=kOutput, calls=%fused_computation.22 | convolution fusion | flops 2822209536 | bytes 22675456 | tf_op jit(solution)/shard_map/dot_general | solution.py:146
  258.0 50.3 %all-gather.10.cloned.1.call-done = bf16[384,4096]{1,0:T(8,128)(2,1)} async-done(((bf16[384,512]{1,0:T(8,128)(2,1)}), bf16[384,4096]{1,0:T(8,128)(2,1)}) %all-gather.10.cloned.1.call-update) | async-done | bytes 3145744 | tf_op jit(solution)/shard_map/all_gather | solution.py:131
  308.2 8.0 %fusion = f32[384,896]{1,0:T(8,128)S(1)} fusion(bf16[384,4096]{1,0:T(8,128)(2,1)} %all-gather.10.cloned.1.call-done, bf16[1,1,4096,896]{3,2,1,0:T(8,128)(2,1)} %param.17), kind=kOutput, calls=%fused_computation.6 | convolution fusion | flops 2818572288 | bytes 11862016 | tf_op jit(solution)/shard_map/dot_general | solution.py:69
  316.2 16.0 %fusion.12 = f32[384,4096]{1,0:T(8,128)} fusion(bf16[1,1,896,4096]{3,2,1,0:T(8,128)(2,1)} %param.19, bf16[384,4096]{1,0:T(8,128)(2,1)} %all-gather.10.cloned.1.call-done, bf16[1,1,4096,896]{3,2,1,0:T(8,128)(2,1)} %param.18, f32[384,896]{1,0:T(8,128)S(1)} %fusion), kind=kOutput, calls=%fused_computation.18 | convolution fusion | flops 5639208960 | bytes 25493504 | tf_op jit(solution)/shard_map/dot_general | solution.py:149
  332.8 4.8 all-to-all-start.3
  337.8 5.0 all-to-all-done.3
  342.8 98.6 %reduce-scatter.3.cloned.1.call-done = f32[384,512]{1,0:T(8,128)} async-done(((f32[384,4096]{1,0:T(8,128)}), f32[384,512]{1,0:T(8,128)}) %reduce-scatter.3.cloned.1.call-update) | async-done | bytes 786448 | tf_op jit(solution)/shard_map/reduce_scatter | solution.py:151
  441.4 4.4 all-to-all-start.2
  446.2 0.5 broadcast.220
  446.7 0.7 reduce.24
  447.5 1.3 gather_fusion.2
  448.8 1.3 gather_fusion.3
  450.0 8.9 %all-to-all-done.2 = f32[8,48,512]{2,1,0:T(8,128)S(1)} async-done(((f32[8,48,512]{2,1,0:T(8,128)}), f32[8,48,512]{2,1,0:T(8,128)S(1)}, u32[]{:S(2)}, u32[]{:S(2)}) %all-to-all-start.2) | async-done | bytes 786464 | tf_op jit(solution)/shard_map/all_to_all | solution.py:155
  458.9 115.4 %reduce-scatter.5.cloned.1.call-done = f32[384,512]{1,0:T(8,128)} async-done(((f32[384,4096]{1,0:T(8,128)}), f32[384,512]{1,0:T(8,128)}) %reduce-scatter.5.cloned.1.call-update) | async-done | bytes 786448 | tf_op jit(solution)/shard_map/reduce_scatter | solution.py:152
  574.3 4.4 all-to-all-start.5
  578.7 0.8 gather_fusion
  579.5 0.8 gather_fusion.1
  580.3 0.5 fusion.45
  580.8 17.6 %all-gather.1 = f32[8,1,128]{2,1,0:T(1,128)S(1)} all-gather(f32[1,1,128]{2,1,0:T(1,128)S(1)} %bitcast.162), channel_id=2, replica_groups=mesh['section'=2,'expert'=8,'hid'=8] {'hid'}, dimensions={0}, use_global_device_ids=true | all-gather | bytes 4608 | tf_op jit(solution)/shard_map/all_gather | solution.py:171
  598.5 0.8 gather_fusion.4
  599.2 0.8 gather_fusion.5
  600.2 3.1 collective-permute-start
  603.3 0.7 select_bitcast_fusion
  603.9 2.8 collective-permute-done
  606.8 0.7 copy.68
  (66 shorter events, 3.5 us)
Async XLA Ops:
  7.2 53.6 %copy-start = (f32[1,512,8]{1,2,0:T(8,128)S(1)}, f32[1,512,8]{1,2,0:T(8,128)}, u32[]{:S(2)}) copy-start(f32[1,512,8]{1,2,0:T(8,128)} %param.16) | copy-start | bytes 49156
  7.2 39.4 %copy-start.3 = (bf16[1,128,512]{2,1,0:T(8,128)(2,1)S(1)}, bf16[1,128,512]{2,1,0:T(8,128)(2,1)}, u32[]{:S(2)}) copy-start(bf16[1,128,512]{2,1,0:T(8,128)(2,1)} %param.11) | copy-start | bytes 393220
  7.2 106.3 %all-gather.8.cloned.1.call-start = ((), (), s32[]{:S(2)}) async-start(), calls=%async_computation.9 | async-start | bytes 3538944 | tf_op jit(solution)/shard_map/all_gather | solution.py:129
  32.3 26.6 %copy-start.5 = (s32[1,128,2]{1,2,0:T(2,128)S(1)}, s32[1,128,2]{1,2,0:T(2,128)}, u32[]{:S(2)}) copy-start(s32[1,128,2]{1,2,0:T(2,128)} %param.14) | copy-start | bytes 3076
  46.5 14.1 %copy-start.2 = (bf16[1,128,512]{2,1,0:T(8,128)(2,1)S(1)}, bf16[1,128,512]{2,1,0:T(8,128)(2,1)}, u32[]{:S(2)}) copy-start(bf16[1,128,512]{2,1,0:T(8,128)(2,1)} %param.12) | copy-start | bytes 393220
  46.5 14.2 %copy-start.1 = (bf16[1,128,512]{2,1,0:T(8,128)(2,1)S(1)}, bf16[1,128,512]{2,1,0:T(8,128)(2,1)}, u32[]{:S(2)}) copy-start(bf16[1,128,512]{2,1,0:T(8,128)(2,1)} %param.10) | copy-start | bytes 393220
  46.5 14.2 %copy-start.4 = (f32[1,512]{1,0:T(1,128)S(1)}, f32[1,512]{1,0:T(1,128)}, u32[]{:S(2)}) copy-start(f32[1,512]{1,0:T(1,128)} %param.15) | copy-start | bytes 6148
  46.5 139.8 %all-gather.6.cloned.1.call-start = ((), (), s32[]{:S(2)}) async-start(), calls=%async_computation.8 | async-start | bytes 3538944 | tf_op jit(solution)/shard_map/all_gather | solution.py:130
  58.9 249.3 %all-gather.10.cloned.1.call-start = ((), (), s32[]{:S(2)}) async-start(), calls=%async_computation.11 | async-start | bytes 3538944 | tf_op jit(solution)/shard_map/all_gather | solution.py:131
  113.5 8.9 %copy-start.6 = (bf16[384,4096]{1,0:T(8,128)(2,1)S(1)}, bf16[384,4096]{1,0:T(8,128)(2,1)}, u32[]{:S(2)}) copy-start(bf16[384,4096]{1,0:T(8,128)(2,1)} %all-gather.8.cloned.1.call-done) | copy-start | bytes 9437188
  241.2 200.2 %reduce-scatter.3.cloned.1.call-start = ((), (), s32[]{:S(2)}) async-start(), calls=%async_computation.10 | async-start | bytes 7077888 | tf_op jit(solution)/shard_map/reduce_scatter | solution.py:151
  257.9 316.3 %reduce-scatter.5.cloned.1.call-start = ((), (), s32[]{:S(2)}) async-start(), calls=%async_computation.12 | async-start | bytes 7077888 | tf_op jit(solution)/shard_map/reduce_scatter | solution.py:152
  332.8 10.0 %all-to-all-start.3 = ((f32[8,48,1]{1,2,0:T(1,128)}), f32[8,48,1]{1,2,0:T(1,128)S(1)}, u32[]{:S(2)}, u32[]{:S(2)}) async-start(f32[8,48,1]{1,2,0:T(1,128)} %bitcast.18), calls=%async_computation.4 | async-start | bytes 8192 | tf_op jit(solution)/shard_map/all_to_all | solution.py:156
  441.4 17.6 %all-to-all-start.2 = ((f32[8,48,512]{2,1,0:T(8,128)}), f32[8,48,512]{2,1,0:T(8,128)S(1)}, u32[]{:S(2)}, u32[]{:S(2)}) async-start(f32[8,48,512]{2,1,0:T(8,128)} %bitcast.155), calls=%async_computation.3 | async-start | bytes 1572864 | tf_op jit(solution)/shard_map/all_to_all | solution.py:155
  574.3 24.2 %all-to-all-start.5 = ((f32[8,48,512]{2,1,0:T(8,128)}), f32[8,48,512]{2,1,0:T(8,128)S(1)}, u32[]{:S(2)}, u32[]{:S(2)}) async-start(f32[8,48,512]{2,1,0:T(8,128)} %bitcast.154), calls=%async_computation.7 | async-start | bytes 1572864 | tf_op jit(solution)/shard_map/all_to_all | solution.py:157
  600.2 6.6 %collective-permute-start = (bf16[128,512]{1,0:T(8,128)(2,1)S(1)}, bf16[128,512]{1,0:T(8,128)(2,1)S(1)}, u32[]{:S(2)}, u32[]{:S(2)}) collective-permute-start(bf16[128,512]{1,0:T(8,128)(2,1)S(1)} %get-tuple-element.18), channel_id=1, source_target_pairs={{0,64},{64,0},{1,65},{65,1},{2,66},{66,2},{3,67},{67,3},{4,68},{68... | collective-permute-start | bytes 393224 | tf_op jit(solution)/shard_map/ppermute | solution.py:18
Sparse Core Ops, SparseCore 0:
  46.7 66.7 all-gather.7
  115.2 71.1 all-gather.5
  241.3 66.9 all-gather.9
  310.5 130.8 reduce-scatter.2
  443.6 130.6 reduce-scatter.4
